TPU v7x, 256 devices: a whole 4x4x8 slice. The times are simulated.
256 devices in a mesh: section: 32 (over z_hi, y, core), fsdp: 8 (over x, z_lo).
Axes of the slice: x: 4, y: 4, z: 8 (z_hi: 4, z_lo: 2; z = z_hi * 2 + z_lo), core: 2. Of those that a mesh axis runs over, the one named last changes fastest.
Arguments:
- acts: bfloat16 [2, 2048, 4096], P(None, 'fsdp'), may hold values from -6 to 6
- gains: float32 [2, 4096], replicated, may hold values from 0.1 to 1.9
- gate_w: bfloat16 [4096, 28672], P('fsdp', 'section'), may hold values from -0.09375 to 0.09375
- up_w: bfloat16 [4096, 28672], P('fsdp', 'section'), may hold values from -0.09375 to 0.09375
- down_w: bfloat16 [28672, 4096], P('section', 'fsdp'), may hold values from -0.046875 to 0.046875
Outputs:
- final_acts: bfloat16 [32, 2048, 4096], P('section', 'fsdp')
All inputs are finite; a program needn't handle non-finite values.
Results may differ from a plain program's by a relative error of at most 0.0047.
Values may be sent and summed in bfloat16 or wider, within the bound.
No kernel may reach another device: no remote copies, remote signals or barrier semaphores. Data moves between devices by JAX's collectives and lax.ppermute only.
A program may use at most 128 MiB of HBM per device.

v0:
```python
import jax
import jax.numpy as jnp
from jax import lax
from jax.sharding import PartitionSpec as P

LAYERS = 2


def swapped(block, axis, stride):
    count = lax.axis_size(axis)
    route = []
    for low in range(count):
        high = low | 1 << stride
        if high != low and high < count:
            route += [(low, high), (high, low)]
    return lax.ppermute(block, axis, route)


def shifted(shard, axis, by):
    length = lax.axis_size(axis)
    return lax.ppermute(shard, axis, [(i, (i + by) % length) for i in range(length)])


def local(acts, gains, gate_w, up_w, down_w):
    group = lax.axis_size("section") // LAYERS
    levels = group.bit_length() - 1
    position = lax.axis_index("section")
    layer = position // group
    state = lax.dynamic_index_in_dim(acts, layer, 0, keepdims=False)
    gain = lax.dynamic_index_in_dim(gains, layer, 0, keepdims=False)
    widened = state.astype(jnp.float32)
    meansq = jnp.mean(widened * widened, axis=-1, keepdims=True)
    normed = (widened * lax.rsqrt(meansq + 1e-05) * gain).astype(jnp.bfloat16)
    gate_panel, up_panel, down_panel = (
        lax.all_gather(gate_w, "fsdp", axis=0, tiled=True),
        lax.all_gather(up_w, "fsdp", axis=0, tiled=True),
        lax.all_gather(down_w, "fsdp", axis=1, tiled=True),
    )
    gate = jnp.dot(normed, gate_panel, preferred_element_type=jnp.float32)
    upper = jnp.dot(normed, up_panel, preferred_element_type=jnp.float32)
    hidden = (jax.nn.silu(gate) * upper).astype(jnp.bfloat16)
    partial_sum = jnp.dot(hidden, down_panel, preferred_element_type=jnp.float32)
    for level in range(levels):
        partial_sum = partial_sum + swapped(partial_sum, "section", level)
    block = (widened + partial_sum).astype(jnp.bfloat16)
    moved = shifted(block, "section", group)
    return moved[None]


def solution(mesh):
    in_specs = (
        P(None, "fsdp", None),
        P(),
        P("fsdp", "section"),
        P("fsdp", "section"),
        P("section", "fsdp"),
    )
    out_specs = P("section", "fsdp", None)
    return jax.shard_map(local, mesh=mesh, in_specs=in_specs, out_specs=out_specs, check_vma=False)
```

profile of v0, /device:TPU:6, one launch (start us, length us, event | category | flops | bytes accessed | tf_op | source)
XLA Modules:
  0.0 968.5 jit_solution(2469996110959038577)
XLA Ops:
  6.5 0.7 all-gather.4.cloned.1.call-update
  7.3 0.7 all-gather.6.cloned.1.call-update
  8.0 0.0 all-gather.8.cloned.1.call-start
  8.1 0.7 all-gather.8.cloned.1.call-update
  8.8 2.1 fusion
  10.9 152.5 %all-gather.4.cloned.1.call-done = bf16[4096,896]{1,0:T(8,128)(2,1)} async-done(((bf16[512,896]{1,0:T(8,128)(2,1)}), bf16[4096,896]{1,0:T(8,128)(2,1)}) %all-gather.4.cloned.1.call-update) | async-done | bytes 7340048 | tf_op jit(solution)/shard_map/all_gather | solution.py:35
  163.4 6.1 fusion.9
  169.5 147.9 %all-gather.6.cloned.1.call-done = bf16[4096,896]{1,0:T(8,128)(2,1)} async-done(((bf16[512,896]{1,0:T(8,128)(2,1)}), bf16[4096,896]{1,0:T(8,128)(2,1)}) %all-gather.6.cloned.1.call-update) | async-done | bytes 7340048 | tf_op jit(solution)/shard_map/all_gather | solution.py:36
  317.5 154.1 %all-gather.8.cloned.1.call-done = bf16[896,4096]{1,0:T(8,128)(2,1)} async-done(((bf16[896,512]{1,0:T(8,128)(2,1)}), bf16[896,4096]{1,0:T(8,128)(2,1)}) %all-gather.8.cloned.1.call-update) | async-done | bytes 7340048 | tf_op jit(solution)/shard_map/all_gather | solution.py:37
  471.6 12.4 %fusion.5 = f32[256,4096]{1,0:T(8,128)} fusion(bf16[896,4096]{1,0:T(8,128)(2,1)} %all-gather.8.cloned.1.call-done, bf16[4096,896]{1,0:T(8,128)(2,1)} %all-gather.6.cloned.1.call-done, f32[256,896]{1,0:T(8,128)S(1)} %fusion.9, f32[4096]{0:T(1024)S(1)} %bitcast.15, f32[256]{0:T(256)S(1)} %add_rsqrt_fusion, bf16[2,256,4096]{2,1,0:T(8,128)(2,1)} %param.5, ...), kind=kOutput, calls=%fused_computation.9 | convolution fusion | flops 3763666944 | bytes 21906436 | tf_op jit(solution)/shard_map/dot_general | solution.py:42
  484.0 7.4 collective-permute-done
  491.3 2.8 add.41
  494.1 1.6 collective-permute-start.1
  495.7 91.1 %collective-permute-done.1 = f32[256,4096]{1,0:T(8,128)S(1)} collective-permute-done((f32[256,4096]{1,0:T(8,128)S(1)}, f32[256,4096]{1,0:T(8,128)S(1)}, u32[]{:S(2)}, u32[]{:S(2)}) %collective-permute-start.1) | collective-permute-done | bytes 4194336 | tf_op jit(solution)/shard_map/ppermute | solution.py:16
  586.8 0.5 add.42
  587.3 3.1 collective-permute-start.2
  590.4 90.3 %collective-permute-done.2 = f32[256,4096]{1,0:T(8,128)S(1)} collective-permute-done((f32[256,4096]{1,0:T(8,128)S(1)}, f32[256,4096]{1,0:T(8,128)S(1)}, u32[]{:S(2)}, u32[]{:S(2)}) %collective-permute-start.2) | collective-permute-done | bytes 4194336 | tf_op jit(solution)/shard_map/ppermute | solution.py:16
  680.7 0.6 add.43
  681.3 2.6 collective-permute-start.3
  683.9 178.9 %collective-permute-done.3 = f32[256,4096]{1,0:T(8,128)S(1)} collective-permute-done((f32[256,4096]{1,0:T(8,128)S(1)}, f32[256,4096]{1,0:T(8,128)S(1)}, u32[]{:S(2)}, u32[]{:S(2)}) %collective-permute-start.3) | collective-permute-done | bytes 4194336 | tf_op jit(solution)/shard_map/ppermute | solution.py:16
  862.8 1.0 fusion.3
  863.8 5.1 collective-permute-start.4
  868.9 91.7 %collective-permute-done.4 = bf16[256,4096]{1,0:T(8,128)(2,1)S(1)} collective-permute-done((bf16[256,4096]{1,0:T(8,128)(2,1)S(1)}, bf16[256,4096]{1,0:T(8,128)(2,1)S(1)}, u32[]{:S(2)}, u32[]{:S(2)}) %collective-permute-start.4) | collective-permute-done | bytes 2097184 | tf_op jit(solution)/shard_map/ppermute | solution.py:21
  960.6 1.3 copy.7
  (11 shorter events, 0.1 us)
Async XLA Ops:
  6.5 4.3 copy-start
  6.5 156.9 %all-gather.4.cloned.1.call-start = ((), (), s32[]{:S(2)}) async-start(), calls=%async_computation | async-start | bytes 8257536 | tf_op jit(solution)/shard_map/all_gather | solution.py:35
  7.3 310.2 %all-gather.6.cloned.1.call-start = ((), (), s32[]{:S(2)}) async-start(), calls=%async_computation.1 | async-start | bytes 8257536 | tf_op jit(solution)/shard_map/all_gather | solution.py:36
  8.0 463.5 %all-gather.8.cloned.1.call-start = ((), (), s32[]{:S(2)}) async-start(), calls=%async_computation.2 | async-start | bytes 8257536 | tf_op jit(solution)/shard_map/all_gather | solution.py:37
  484.0 7.4 collective-permute-start
  494.1 92.7 %collective-permute-start.1 = (f32[256,4096]{1,0:T(8,128)S(1)}, f32[256,4096]{1,0:T(8,128)S(1)}, u32[]{:S(2)}, u32[]{:S(2)}) collective-permute-start(f32[256,4096]{1,0:T(8,128)S(1)} %add.41), channel_id=1, source_target_pairs={{0,16},{16,0},{8,24},{24,8},{32,48},{48,32},{40,56},{56,40},{64,80... | collective-permute-start | bytes 12582920 | tf_op jit(solution)/shard_map/ppermute | solution.py:16
  587.3 275.5 %copy-start.2 = (bf16[2,256,4096]{2,1,0:T(8,128)(2,1)S(1)}, bf16[2,256,4096]{2,1,0:T(8,128)(2,1)}, u32[]{:S(2)}) copy-start(bf16[2,256,4096]{2,1,0:T(8,128)(2,1)} %param.5) | copy-start | bytes 12582916
  587.3 93.4 %collective-permute-start.2 = (f32[256,4096]{1,0:T(8,128)S(1)}, f32[256,4096]{1,0:T(8,128)S(1)}, u32[]{:S(2)}, u32[]{:S(2)}) collective-permute-start(f32[256,4096]{1,0:T(8,128)S(1)} %add.42), channel_id=1, source_target_pairs={{0,32},{32,0},{8,40},{40,8},{16,48},{48,16},{24,56},{56,24},{64,96... | collective-permute-start | bytes 12582920 | tf_op jit(solution)/shard_map/ppermute | solution.py:16
  681.3 181.5 %collective-permute-start.3 = (f32[256,4096]{1,0:T(8,128)S(1)}, f32[256,4096]{1,0:T(8,128)S(1)}, u32[]{:S(2)}, u32[]{:S(2)}) collective-permute-start(f32[256,4096]{1,0:T(8,128)S(1)} %add.43), channel_id=1, source_target_pairs={{0,64},{64,0},{8,72},{72,8},{16,80},{80,16},{24,88},{88,24},{32,96... | collective-permute-start | bytes 12582920 | tf_op jit(solution)/shard_map/ppermute | solution.py:16
  862.8 99.1 %copy-start.1 = (f32[2,4096]{1,0:T(2,128)S(1)}, f32[2,4096]{1,0:T(2,128)}, u32[]{:S(2)}) copy-start(f32[2,4096]{1,0:T(2,128)} %param.6) | copy-start | bytes 98308
  863.8 96.8 %collective-permute-start.4 = (bf16[256,4096]{1,0:T(8,128)(2,1)S(1)}, bf16[256,4096]{1,0:T(8,128)(2,1)S(1)}, u32[]{:S(2)}, u32[]{:S(2)}) collective-permute-start(bf16[256,4096]{1,0:T(8,128)(2,1)S(1)} %fusion.3), channel_id=1, source_target_pairs={{0,128},{8,136},{16,144},{24,152},{32,160},{40,168},{48,176},{56,1... | collective-permute-start | bytes 6291464 | tf_op jit(solution)/shard_map/ppermute | solution.py:21
Sparse Core Ops, SparseCore 0:
  9.1 154.2 all-gather.3
  165.2 152.2 all-gather.5
  319.3 152.2 all-gather.7
where the time goes:
time: 969 us; the launch traced here: 968 us
  waiting for transfers between devices  916 us (95%)
  matrix products  18.5 us (2%)
  between operations  13.2 us (1%)
  starting transfers between devices  12.5 us (1%)
    ppermute x4, waiting for transfers between devices, swapped(): return lax.ppermute(block, axis, route)  368 us
    all_gather x1, waiting for transfers between devices, local(): lax.all_gather(down_w, 'fsdp', axis=1, tiled=True)  154 us
    all_gather x1, waiting for transfers between devices, local(): lax.all_gather(gate_w, 'fsdp', axis=0, tiled=True)  153 us
    all_gather x1, waiting for transfers between devices, local(): lax.all_gather(up_w, 'fsdp', axis=0, tiled=True)  148 us
    ppermute x1, waiting for transfers between devices, shifted(): lax.ppermute(shard, axis, [(i, (i + by) % length) for i in range(length)])  91.7 us
  transfers between devices with their start and end apart: 8, of which 8 were waited for; matrix products, arithmetic and copies ran while one was open for 1% of the time, Pallas kernels for 0%

commit v1 on v0

--- a/solution.py
+++ b/solution.py
@@ -31,9 +31,22 @@
     widened = state.astype(jnp.float32)
     meansq = jnp.mean(widened * widened, axis=-1, keepdims=True)
     normed = (widened * lax.rsqrt(meansq + 1e-05) * gain).astype(jnp.bfloat16)
+
+    def use_panels_by_axis(payload):
+        mat_out = jnp.concatenate(
+            jax.lax.all_to_all(
+                jnp.stack([payload] * jax.lax.psum(1, axis_name="fsdp"), axis=0),
+                axis_name="fsdp",
+                split_axis=0,
+                concat_axis=0,
+            ),
+            axis=0,
+        )
+        return mat_out
+
     gate_panel, up_panel, down_panel = (
         lax.all_gather(gate_w, "fsdp", axis=0, tiled=True),
-        lax.all_gather(up_w, "fsdp", axis=0, tiled=True),
+        use_panels_by_axis(up_w),
         lax.all_gather(down_w, "fsdp", axis=1, tiled=True),
     )
     gate = jnp.dot(normed, gate_panel, preferred_element_type=jnp.float32)

time: 969 us -> 890 us (0.918)
  waiting for transfers between devices: 916 us -> 825 us
    all_gather x1 -> x0, waiting for transfers between devices: 148 us -> none  [local(): lax.all_gather(up_w, 'fsdp', axis=0, tiled=True)]
    all_gather x1, waiting for transfers between devices: 153 us -> 215 us  [local(): lax.all_gather(gate_w, 'fsdp', axis=0, tiled=True)]
  transfers between devices with their start and end apart: 8 -> 8, of which waited for: 8 -> 7; matrix products, arithmetic and copies ran while one was open for 1% -> 1% of each run, Pallas kernels for 0% -> 0%
where the time goes in v1:
time: 890 us
  waiting for transfers between devices  825 us (93%)
  starting transfers between devices  19.4 us (2%)
  matrix products  18.5 us (2%)
  between operations  13.5 us (2%)
    ppermute x4, waiting for transfers between devices, swapped(): return lax.ppermute(block, axis, route)  368 us
    all_gather x1, waiting for transfers between devices, local(): lax.all_gather(gate_w, 'fsdp', axis=0, tiled=True)  215 us
    all_gather x1, waiting for transfers between devices, local(): lax.all_gather(down_w, 'fsdp', axis=1, tiled=True)  149 us
    ppermute x1, waiting for transfers between devices, shifted(): lax.ppermute(shard, axis, [(i, (i + by) % length) for i in range(length)])  91.7 us
  transfers between devices with their start and end apart: 8, of which 7 were waited for; matrix products, arithmetic and copies ran while one was open for 1% of the time, Pallas kernels for 0%

profile of v1, /device:TPU:6, one launch (start us, length us, event | category | flops | bytes accessed | tf_op | source)
XLA Modules:
  0.0 889.8 jit_solution(10779722085936495110)
XLA Ops:
  6.5 0.7 all-gather.3.cloned.1.call-update
  7.3 5.1 stack.2
  12.3 7.0 all-to-all-start
  19.3 0.7 all-gather.5.cloned.1.call-update
  20.1 2.1 fusion.3
  22.2 214.9 %all-gather.3.cloned.1.call-done = bf16[4096,896]{1,0:T(8,128)(2,1)} async-done(((bf16[512,896]{1,0:T(8,128)(2,1)}), bf16[4096,896]{1,0:T(8,128)(2,1)}) %all-gather.3.cloned.1.call-update) | async-done | bytes 7340048 | tf_op jit(solution)/shard_map/all_gather | solution.py:48
  237.1 6.1 fusion.12
  243.3 149.3 %all-gather.5.cloned.1.call-done = bf16[896,4096]{1,0:T(8,128)(2,1)} async-done(((bf16[896,512]{1,0:T(8,128)(2,1)}), bf16[896,4096]{1,0:T(8,128)(2,1)}) %all-gather.5.cloned.1.call-update) | async-done | bytes 7340048 | tf_op jit(solution)/shard_map/all_gather | solution.py:50
  392.6 12.4 %fusion.27 = f32[256,4096]{1,0:T(8,128)} fusion(bf16[896,4096]{1,0:T(8,128)(2,1)} %all-gather.5.cloned.1.call-done, bf16[4096,896]{1,0:T(8,128)(2,1)} %bitcast.3, f32[4096]{0:T(1024)S(1)} %bitcast.34, f32[256]{0:T(256)S(1)} %add_rsqrt_fusion, bf16[2,256,4096]{2,1,0:T(8,128)(2,1)} %param.5, s32[]{:T(128)S(6)} %select_n.12, f32[256,896]{1,0:T(8,128)S(1)} %fusion.12), kind=kOutput, calls=%fused_computation.22 | convolution fusion | flops 3763666944 | bytes 21906436 | tf_op jit(solution)/shard_map/dot_general | solution.py:55
  405.0 7.4 collective-permute-done
  412.4 2.8 add.41
  415.1 1.6 collective-permute-start.1
  416.7 91.1 %collective-permute-done.1 = f32[256,4096]{1,0:T(8,128)S(1)} collective-permute-done((f32[256,4096]{1,0:T(8,128)S(1)}, f32[256,4096]{1,0:T(8,128)S(1)}, u32[]{:S(2)}, u32[]{:S(2)}) %collective-permute-start.1) | collective-permute-done | bytes 4194336 | tf_op jit(solution)/shard_map/ppermute | solution.py:16
  507.8 0.5 add.42
  508.3 0.0 copy-start.2
  508.3 3.1 collective-permute-start.2
  511.5 90.3 %collective-permute-done.2 = f32[256,4096]{1,0:T(8,128)S(1)} collective-permute-done((f32[256,4096]{1,0:T(8,128)S(1)}, f32[256,4096]{1,0:T(8,128)S(1)}, u32[]{:S(2)}, u32[]{:S(2)}) %collective-permute-start.2) | collective-permute-done | bytes 4194336 | tf_op jit(solution)/shard_map/ppermute | solution.py:16
  601.7 0.6 add.43
  602.3 2.6 collective-permute-start.3
  604.9 178.9 %collective-permute-done.3 = f32[256,4096]{1,0:T(8,128)S(1)} collective-permute-done((f32[256,4096]{1,0:T(8,128)S(1)}, f32[256,4096]{1,0:T(8,128)S(1)}, u32[]{:S(2)}, u32[]{:S(2)}) %collective-permute-start.3) | collective-permute-done | bytes 4194336 | tf_op jit(solution)/shard_map/ppermute | solution.py:16
  783.8 1.0 fusion.6
  784.8 5.1 collective-permute-start.4
  789.9 91.7 %collective-permute-done.4 = bf16[256,4096]{1,0:T(8,128)(2,1)S(1)} collective-permute-done((bf16[256,4096]{1,0:T(8,128)(2,1)S(1)}, bf16[256,4096]{1,0:T(8,128)(2,1)S(1)}, u32[]{:S(2)}, u32[]{:S(2)}) %collective-permute-start.4) | collective-permute-done | bytes 2097184 | tf_op jit(solution)/shard_map/ppermute | solution.py:21
  881.7 1.3 copy.7
  (11 shorter events, 0.0 us)
Async XLA Ops:
  6.5 15.6 %copy-start = (f32[2,4096]{1,0:T(2,128)S(1)}, f32[2,4096]{1,0:T(2,128)}, u32[]{:S(2)}) copy-start(f32[2,4096]{1,0:T(2,128)} %param.6) | copy-start | bytes 98308
  6.5 230.6 %all-gather.3.cloned.1.call-start = ((), (), s32[]{:S(2)}) async-start(), calls=%async_computation.1 | async-start | bytes 8257536 | tf_op jit(solution)/shard_map/all_gather | solution.py:48
  12.3 230.9 %all-to-all-start = ((bf16[8,512,896]{2,1,0:T(8,128)(2,1)}), bf16[8,512,896]{2,1,0:T(8,128)(2,1)}, u32[]{:S(2)}, u32[]{:S(2)}) async-start(bf16[8,512,896]{2,1,0:T(8,128)(2,1)} %stack.2), calls=%async_computation | async-start | bytes 14680064 | tf_op jit(solution)/shard_map/all_to_all | solution.py:37
  19.3 373.3 %all-gather.5.cloned.1.call-start = ((), (), s32[]{:S(2)}) async-start(), calls=%async_computation.2 | async-start | bytes 8257536 | tf_op jit(solution)/shard_map/all_gather | solution.py:50
  405.0 7.4 collective-permute-start
  415.1 92.7 %collective-permute-start.1 = (f32[256,4096]{1,0:T(8,128)S(1)}, f32[256,4096]{1,0:T(8,128)S(1)}, u32[]{:S(2)}, u32[]{:S(2)}) collective-permute-start(f32[256,4096]{1,0:T(8,128)S(1)} %add.41), channel_id=1, source_target_pairs={{0,16},{16,0},{8,24},{24,8},{32,48},{48,32},{40,56},{56,40},{64,80... | collective-permute-start | bytes 12582920 | tf_op jit(solution)/shard_map/ppermute | solution.py:16
  508.3 275.5 %copy-start.2 = (bf16[2,256,4096]{2,1,0:T(8,128)(2,1)S(1)}, bf16[2,256,4096]{2,1,0:T(8,128)(2,1)}, u32[]{:S(2)}) copy-start(bf16[2,256,4096]{2,1,0:T(8,128)(2,1)} %param.5) | copy-start | bytes 12582916
  508.3 93.4 %collective-permute-start.2 = (f32[256,4096]{1,0:T(8,128)S(1)}, f32[256,4096]{1,0:T(8,128)S(1)}, u32[]{:S(2)}, u32[]{:S(2)}) collective-permute-start(f32[256,4096]{1,0:T(8,128)S(1)} %add.42), channel_id=1, source_target_pairs={{0,32},{32,0},{8,40},{40,8},{16,48},{48,16},{24,56},{56,24},{64,96... | collective-permute-start | bytes 12582920 | tf_op jit(solution)/shard_map/ppermute | solution.py:16
  602.3 181.5 %collective-permute-start.3 = (f32[256,4096]{1,0:T(8,128)S(1)}, f32[256,4096]{1,0:T(8,128)S(1)}, u32[]{:S(2)}, u32[]{:S(2)}) collective-permute-start(f32[256,4096]{1,0:T(8,128)S(1)} %add.43), channel_id=1, source_target_pairs={{0,64},{64,0},{8,72},{72,8},{16,80},{80,16},{24,88},{88,24},{32,96... | collective-permute-start | bytes 12582920 | tf_op jit(solution)/shard_map/ppermute | solution.py:16
  783.8 99.1 %copy-start.1 = (f32[2,4096]{1,0:T(2,128)S(1)}, f32[2,4096]{1,0:T(2,128)}, u32[]{:S(2)}) copy-start(f32[2,4096]{1,0:T(2,128)} %param.6) | copy-start | bytes 98308
  784.8 96.8 %collective-permute-start.4 = (bf16[256,4096]{1,0:T(8,128)(2,1)S(1)}, bf16[256,4096]{1,0:T(8,128)(2,1)S(1)}, u32[]{:S(2)}, u32[]{:S(2)}) collective-permute-start(bf16[256,4096]{1,0:T(8,128)(2,1)S(1)} %fusion.6), channel_id=1, source_target_pairs={{0,128},{8,136},{16,144},{24,152},{32,160},{40,168},{48,176},{56,1... | collective-permute-start | bytes 6291464 | tf_op jit(solution)/shard_map/ppermute | solution.py:21
Sparse Core Ops, SparseCore 0:
  9.1 227.9 all-gather.2
  238.9 153.6 all-gather.4
